TPU v7x, 32 devices: a whole 2x2x4 slice. The times are simulated.
32 devices in a mesh: groups: 2 (over y), servers: 4 (over z), heads: 4 (over x, core).
Axes of the slice: x: 2, y: 2, z: 4, core: 2. Of those that a mesh axis runs over, the one named last changes fastest.
Arguments:
- grad_out: bfloat16 [4096, 2048], P(('groups', 'servers')), parts along dimension 0, may hold values from -6 to 6
- out_weight: bfloat16 [2048, 4096], P(None, 'heads'), may hold values from -0.125 to 0.125
- queries: bfloat16 [4096, 4096], P(('groups', 'servers'), 'heads'), parts along dimension 0, may hold values from -2.5 to 2.5
- attn_out: bfloat16 [4096, 4096], P(('groups', 'servers'), 'heads'), parts along dimension 0, may hold values from -4 to 4
- lse: float32 [32, 4096], P('heads', ('groups', 'servers')), parts along dimension 1, may hold values from 5 to 6.5
- keys: bfloat16 [4096, 512], P(('groups', 'servers'), 'heads'), parts along dimension 0, may hold values from -2.5 to 2.5
- values: bfloat16 [4096, 512], P(('groups', 'servers'), 'heads'), parts along dimension 0, may hold values from -4 to 4
- prefix_keys: bfloat16 [256, 512], P(('groups', 'servers'), 'heads'), parts along dimension 0, may hold values from -2.5 to 2.5
- prefix_values: bfloat16 [256, 512], P(('groups', 'servers'), 'heads'), parts along dimension 0, may hold values from -4 to 4
- fork_owner: int32 [128, 1], P('groups'), parts along dimension 0, may hold values from 0 to 3; in each aligned block of 16 rows (0 to 15, 16 to 31, ...) at most 8 rows name the same one
- fork_root: int32 [128], P('groups'), parts along dimension 0, may hold values from 0 to 3
- fork_offset: int32 [128], P('groups'), parts along dimension 0, may hold values from 1 to 64
Outputs:
- grad_queries: bfloat16 [4096, 4096], P(('groups', 'servers'), 'heads'), parts along dimension 0
- grad_keys: bfloat16 [4096, 512], P(('groups', 'servers'), 'heads'), parts along dimension 0
- grad_values: bfloat16 [4096, 512], P(('groups', 'servers'), 'heads'), parts along dimension 0
- prefix_grad_keys: bfloat16 [256, 512], P(('groups', 'servers'), 'heads'), parts along dimension 0
- prefix_grad_values: bfloat16 [256, 512], P(('groups', 'servers'), 'heads'), parts along dimension 0
There are 2 independent parts, one for each index of `groups`. A program takes and returns all parts, laid end to end along the dimension named above; an argument that names none is the same for every part. Nothing has to cross between parts.
Inputs may be any that keep to these rules, and one draw needn't show every extreme that they name: `fork_owner`: row g names the owner of the rollout that continuation g forks from. Among the continuations of one owner (aligned blocks of 16 rows) no owner is named more than 8 times.
All inputs are finite; a program needn't handle non-finite values.
Results may differ from a plain program's by a relative error of at most 0.0061.
Values may be sent and summed in bfloat16 or wider, within the bound.
No kernel may reach another device: no remote copies, remote signals or barrier semaphores. Data moves between devices by JAX's collectives and lax.ppermute only.
A program may use at most 128 MiB of HBM per device.

v0:
```python
import math
import jax
import jax.numpy as jnp
from jax import lax
from jax.sharding import PartitionSpec as P

HD = 128
CH_DEV = 16
ROOTS_DEV = 4
RLEN = 64
CLEN = 16


def attend(query_heads, out_heads, lse_rows, delta_rows, key_heads, value_heads, mask_rows):
    tok_count, head_local, head_size = query_heads.shape
    key_count, shared_heads, _ = key_heads.shape
    group_size = head_local // shared_heads
    scaling = head_size ** (-0.5)
    block_rows = math.gcd(tok_count, 128)
    block_count = tok_count // block_rows
    contract = (((1,), (1,)), ((), ()))
    across = (((0,), (0,)), ((), ()))
    key_list = [key_heads[:, 0]]
    value_list = [value_heads[:, 0]]

    def block_step(totals, block_index):
        key_totals, value_totals = totals
        start = block_index * block_rows
        query_block = lax.dynamic_slice_in_dim(query_heads, start, block_rows, 0).reshape(
            block_rows, shared_heads, group_size, head_size
        )
        out_block = lax.dynamic_slice_in_dim(out_heads, start, block_rows, 0).reshape(
            block_rows, shared_heads, group_size, head_size
        )
        lse_block = lax.dynamic_slice_in_dim(lse_rows, start, block_rows, 1).reshape(
            shared_heads, group_size, block_rows
        )
        delta_block = lax.dynamic_slice_in_dim(delta_rows, start, block_rows, 1).reshape(
            shared_heads, group_size, block_rows
        )
        allowed = mask_rows(start, block_rows)
        allowed_wide = jnp.broadcast_to(
            allowed[:, None, :], (block_rows, group_size, key_count)
        ).reshape(block_rows * group_size, key_count)
        query_flat = query_block[:, 0].reshape(block_rows * group_size, head_size)
        out_flat = out_block[:, 0].reshape(block_rows * group_size, head_size)
        lse_flat = jnp.transpose(lse_block[0]).reshape(-1)
        delta_flat = jnp.transpose(delta_block[0]).reshape(-1)
        scores = (
            lax.dot_general(query_flat, key_list[0], contract, preferred_element_type=jnp.float32)
            * scaling
        )
        weights = jnp.where(allowed_wide, jnp.exp(scores - lse_flat[:, None]), jnp.float32(0.0))
        weights_low = weights.astype(jnp.bfloat16)
        weight_grads = lax.dot_general(
            out_flat, value_list[0], contract, preferred_element_type=jnp.float32
        )
        score_grads = (weights * (weight_grads - delta_flat[:, None])).astype(jnp.bfloat16)
        grad_query = jnp.dot(score_grads, key_list[0], preferred_element_type=jnp.float32) * scaling
        query_parts = [grad_query.reshape(block_rows, group_size, head_size)]
        new_keys = [
            lax.dot_general(score_grads, query_flat, across, preferred_element_type=jnp.float32)
            * scaling
        ]
        new_values = [
            lax.dot_general(weights_low, out_flat, across, preferred_element_type=jnp.float32)
        ]
        key_totals = key_totals + jnp.stack(new_keys, axis=1)
        value_totals = value_totals + jnp.stack(new_values, axis=1)
        grad_block = jnp.stack(query_parts, axis=1).reshape(block_rows, head_local, head_size)
        return ((key_totals, value_totals), grad_block)

    empty_grads = jnp.zeros(key_heads.shape, jnp.float32)
    totals, query_grads = lax.scan(
        block_step, (empty_grads, empty_grads), jnp.arange(block_count, dtype=jnp.int32)
    )
    return (query_grads.reshape(tok_count, head_local, head_size), totals[0], totals[1])


def local(
    grad_out,
    out_weight,
    queries,
    attn_out,
    lse,
    keys,
    values,
    prefix_keys,
    prefix_values,
    fork_owner,
    fork_root,
    fork_offset,
):
    tok_rows = queries.shape[0]
    head_local = lse.shape[0]
    shared_heads = keys.shape[1] // HD
    shared_width = keys.shape[1]
    servers_count = lax.axis_size("servers")
    my_index = lax.axis_index("servers")
    root_rows = ROOTS_DEV * RLEN
    out_grad = jnp.dot(grad_out, out_weight, preferred_element_type=jnp.float32).astype(
        jnp.bfloat16
    )
    out_heads = out_grad.reshape(tok_rows, head_local, HD)
    query_heads = queries.reshape(tok_rows, head_local, HD)
    output_heads = attn_out.reshape(tok_rows, head_local, HD)
    delta_rows = jnp.transpose(
        jnp.sum(out_heads.astype(jnp.float32) * output_heads.astype(jnp.float32), axis=2)
    )
    key_heads = keys.reshape(tok_rows, shared_heads, HD)
    value_heads = values.reshape(tok_rows, shared_heads, HD)
    gathered = (
        lax.all_gather(prefix_keys, "servers", axis=0, tiled=True),
        lax.all_gather(prefix_values, "servers", axis=0, tiled=True),
    )
    prompt_keys = gathered[0].reshape(-1, shared_heads, HD)
    prompt_values = gathered[1].reshape(-1, shared_heads, HD)
    prompt_count = prompt_keys.shape[0]

    def open_rows(start, rows):
        return jnp.ones((rows, prompt_count), dtype=jnp.bool_)

    pre_query_grad, pre_key_grad, pre_value_grad = attend(
        query_heads, out_heads, lse, delta_rows, prompt_keys, prompt_values, open_rows
    )
    prompt_sums = (
        lax.psum_scatter(
            pre_key_grad.reshape(-1, shared_width), "servers", scatter_dimension=0, tiled=True
        ),
        lax.psum_scatter(
            pre_value_grad.reshape(-1, shared_width), "servers", scatter_dimension=0, tiled=True
        ),
    )
    local_index = jnp.arange(tok_rows, dtype=jnp.int32)
    child_part = local_index - root_rows
    in_root = local_index < root_rows
    segment_ids = jnp.where(in_root, local_index // RLEN, ROOTS_DEV + child_part // CLEN)
    segment_pos = jnp.where(in_root, local_index % RLEN, child_part % CLEN)

    def own_rows(start, rows):
        query_seg = lax.dynamic_slice_in_dim(segment_ids, start, rows, 0)
        query_pos = lax.dynamic_slice_in_dim(segment_pos, start, rows, 0)
        return (query_seg[:, None] == segment_ids[None, :]) & (
            segment_pos[None, :] <= query_pos[:, None]
        )

    local_query_grad, local_key_grad, local_value_grad = attend(
        query_heads, out_heads, lse, delta_rows, key_heads, value_heads, own_rows
    )
    child_query = query_heads[root_rows:]
    child_out = out_heads[root_rows:]
    child_lse = lse[:, root_rows:]
    child_delta = delta_rows[:, root_rows:]
    owners_all = fork_owner[:, 0].reshape(servers_count, CH_DEV)
    roots_all = fork_root.reshape(servers_count, CH_DEV)
    my_owners = lax.dynamic_index_in_dim(owners_all, my_index, 0, keepdims=False)
    my_roots = lax.dynamic_index_in_dim(roots_all, my_index, 0, keepdims=False)
    my_offsets = lax.dynamic_slice_in_dim(fork_offset, my_index * CH_DEV, CH_DEV, 0)
    positions = jnp.arange(RLEN, dtype=jnp.int32)
    parent_key_index = jnp.arange(CH_DEV * RLEN, dtype=jnp.int32)
    parent_slot = parent_key_index // RLEN
    parent_pos = parent_key_index % RLEN

    def parent_rows(start, rows):
        child_ids = (start + jnp.arange(rows, dtype=jnp.int32)) // CLEN
        child_limit = jnp.take(my_offsets, child_ids, axis=0)
        return (child_ids[:, None] == parent_slot[None, :]) & (
            parent_pos[None, :] < child_limit[:, None]
        )

    root_keys = keys[:root_rows]
    root_values = values[:root_rows]
    all_roots = (
        lax.all_gather(root_keys, "servers", axis=0, tiled=True),
        lax.all_gather(root_values, "servers", axis=0, tiled=True),
    )
    parent_index = ((my_owners * ROOTS_DEV + my_roots) * RLEN)[:, None] + positions[None, :]
    flat_index = parent_index.reshape(-1)
    parent_keys = jnp.take(all_roots[0], flat_index, axis=0).reshape(
        CH_DEV * RLEN, shared_heads, HD
    )
    parent_values = jnp.take(all_roots[1], flat_index, axis=0).reshape(
        CH_DEV * RLEN, shared_heads, HD
    )
    parent_query_grad, parent_key_grad, parent_value_grad = attend(
        child_query, child_out, child_lse, child_delta, parent_keys, parent_values, parent_rows
    )
    dense_keys = (
        jnp.zeros((all_roots[0].shape[0], shared_width), jnp.float32)
        .at[flat_index]
        .add(parent_key_grad.reshape(-1, shared_width))
    )
    dense_values = (
        jnp.zeros((all_roots[1].shape[0], shared_width), jnp.float32)
        .at[flat_index]
        .add(parent_value_grad.reshape(-1, shared_width))
    )
    root_sums = (
        lax.psum_scatter(dense_keys, "servers", scatter_dimension=0, tiled=True),
        lax.psum_scatter(dense_values, "servers", scatter_dimension=0, tiled=True),
    )
    root_key_part = root_sums[0]
    root_value_part = root_sums[1]
    own_query_grad = pre_query_grad + local_query_grad
    grad_query = jnp.concatenate(
        [own_query_grad[:root_rows], own_query_grad[root_rows:] + parent_query_grad], axis=0
    )
    grad_queries = grad_query.astype(jnp.bfloat16).reshape(tok_rows, head_local * HD)
    local_keys = local_key_grad.reshape(tok_rows, shared_width)
    local_values = local_value_grad.reshape(tok_rows, shared_width)
    grad_keys = jnp.concatenate(
        [local_keys[:root_rows] + root_key_part, local_keys[root_rows:]], axis=0
    ).astype(jnp.bfloat16)
    grad_values = jnp.concatenate(
        [local_values[:root_rows] + root_value_part, local_values[root_rows:]], axis=0
    ).astype(jnp.bfloat16)
    prefix_grad_keys = prompt_sums[0].astype(jnp.bfloat16)
    prefix_grad_values = prompt_sums[1].astype(jnp.bfloat16)
    return (grad_queries, grad_keys, grad_values, prefix_grad_keys, prefix_grad_values)


def solution(mesh):
    placed = (
        P(("groups", "servers"), None),
        P(None, "heads"),
        P(("groups", "servers"), "heads"),
        P(("groups", "servers"), "heads"),
        P("heads", ("groups", "servers")),
        P(("groups", "servers"), "heads"),
        P(("groups", "servers"), "heads"),
        P(("groups", "servers"), "heads"),
        P(("groups", "servers"), "heads"),
        P("groups", None),
        P("groups"),
        P("groups"),
    )
    return jax.shard_map(
        local,
        mesh=mesh,
        in_specs=placed,
        out_specs=(
            P(("groups", "servers"), "heads"),
            P(("groups", "servers"), "heads"),
            P(("groups", "servers"), "heads"),
            P(("groups", "servers"), "heads"),
            P(("groups", "servers"), "heads"),
        ),
        check_vma=False,
    )
```

profile of v0, /device:TPU:0, one launch (start us, length us, event | category | flops | bytes accessed | tf_op | source)
XLA Modules:
  0.0 282.1 jit_solution(4056299993716482109)
XLA Ops:
  8.8 4.5 %convolution_convert_fusion = bf16[512,1024]{1,0:T(8,128)(2,1)S(1)} fusion(bf16[512,2048]{1,0:T(8,128)(2,1)S(1)} %copy-done, bf16[2048,1024]{1,0:T(8,128)(2,1)} %param.21), kind=kOutput, calls=%fused_computation.132 | convolution fusion | flops 2148007936 | bytes 7340032 | tf_op jit(solution)/shard_map/dot_general | solution.py:101
  20.3 14.8 %all_gather.12 = bf16[128,128]{1,0:T(8,128)(2,1)S(1)} all-gather(bf16[32,128]{1,0:T(8,128)(2,1)S(1)} %copy-done.16), channel_id=1, replica_groups=mesh['groups'=2,'servers'=4,'heads'=4] {'servers'}, dimensions={0}, use_global_device_ids=true | all-gather | bytes 40960 | tf_op jit(solution)/shard_map/all_gather | solution.py:113
  35.1 13.1 %all_gather.13 = bf16[128,128]{1,0:T(8,128)(2,1)S(1)} all-gather(bf16[32,128]{1,0:T(8,128)(2,1)S(1)} %copy-done.17), channel_id=1, replica_groups=mesh['groups'=2,'servers'=4,'heads'=4] {'servers'}, dimensions={0}, use_global_device_ids=true | all-gather | bytes 40960 | tf_op jit(solution)/shard_map/all_gather | solution.py:114
  52.2 34.4 %while.48 = (s32[]{:T(128)}, f32[128,1,128]{2,0,1:T(8,128)}, f32[128,1,128]{2,0,1:T(8,128)}, f32[4,128,8,128]{3,2,1,0:T(8,128)}, s32[4]{0:T(128)S(1)}, /*index=5...) while((s32[]{:T(128)}, f32[128,1,128]{2,0,1:T(8,128)}, ...), condition=%wide.region_2.3_spmd.clone, body=%wide.region_1.2_spmd.clone.sunk | while | flops 168771584 | bytes 4334310 | solution.py:74
  94.1 14.2 %all_gather.14 = bf16[1024,128]{1,0:T(8,128)(2,1)S(1)} all-gather(bf16[256,128]{1,0:T(8,128)(2,1)S(1)} %slice-done.1), channel_id=1, replica_groups=mesh['groups'=2,'servers'=4,'heads'=4] {'servers'}, dimensions={0}, use_global_device_ids=true | all-gather | bytes 327680 | tf_op jit(solution)/shard_map/all_gather | solution.py:174
  108.3 14.1 %all_gather.15 = bf16[1024,128]{1,0:T(8,128)(2,1)S(1)} all-gather(bf16[256,128]{1,0:T(8,128)(2,1)S(1)} %slice-done), channel_id=1, replica_groups=mesh['groups'=2,'servers'=4,'heads'=4] {'servers'}, dimensions={0}, use_global_device_ids=true | all-gather | bytes 327680 | tf_op jit(solution)/shard_map/all_gather | solution.py:175
  122.3 4.3 %gather_fusion = bf16[1024,128]{1,0:T(8,128)(2,1)} fusion(bf16[1024,128]{1,0:T(8,128)(2,1)S(1)} %all_gather.14, s32[1024]{0:T(1024)S(1)} %fusion.100), kind=kCustom, calls=%fused_computation.clone | custom fusion | bytes 528384 | tf_op jit(solution)/shard_map/jit(_take)/gather | solution.py:179
  126.6 4.3 %gather_fusion.1 = bf16[1024,128]{1,0:T(8,128)(2,1)} fusion(bf16[1024,128]{1,0:T(8,128)(2,1)S(1)} %all_gather.15, s32[1024]{0:T(1024)S(1)} %fusion.100), kind=kCustom, calls=%fused_computation.1.clone | custom fusion | bytes 528384 | tf_op jit(solution)/shard_map/jit(_take)/gather | solution.py:182
  136.1 56.4 %while.49 = (s32[]{:T(128)}, f32[1024,1,128]{2,0,1:T(8,128)S(1)}, f32[1024,1,128]{2,0,1:T(8,128)}, f32[2,128,8,128]{3,2,1,0:T(8,128)}, s32[2]{0:T(128)S(1)}, /*i...) while((s32[]{:T(128)}, f32[1024,1,128]{2,0,1:T(8,128)S(1)}, ...), condition=%wide.region_6.8_spmd.clone, body=%wide.region_5.7_spmd.clone.sunk | while | flops 1353864192 | bytes 51641432 | solution.py:74
  138.0 10.0 %and_select_fusion.4 = (s32[128]{0:T(128)S(1)}, s32[128]{0:T(128)S(1)}) fusion(s32[]{:T(128)} %bitcast.344, s32[]{:T(128)} %bitcast.345, s32[]{:T(128)} %bitcast.346, s32[]{:T(128)} %bitcast.347, s32[]{:T(128)} %bitcast.348, s32[]{:T(128)} %bitcast.349, s32[]{:T(128)} %bitcast.350, s32[]{:T(128)} %bitcast.351, s32[]{:T(128)} %bitcast.352, ...), kind=kLoop, calls=%fused_computation.89.clone.1 | loop fusion | flops 9216 | bytes 1092 | tf_op jit(solution)/shard_map/while/body/eval_jaxpr/jit(_take)/select_n | solution.py:166
  151.8 3.9 %multiply_convert_fusion.4 = bf16[1024,1024]{1,0:T(8,128)(2,1)S(1)} fusion(f32[1024,1024]{1,0:T(8,128)} %fusion.196, bf16[1024,128]{1,0:T(8,128)(2,1)} %get-tuple-element.918, f32[1024]{0:T(1024)S(1)} %sub.266, f32[1024]{0:T(1024)S(1)} %sub.267, pred[128,1024]{1,0:T(8,128)(4,1)} %compare_and_fusion.5, bf16[256,8,128]{2,1,0:T(8,128)(2,1)} %get-tuple-element.917, ...), kind=kOutput, calls=%fused_computation.35.clone.1 | convolution fusion | flops 274726912 | bytes 6955012 | tf_op jit(solution)/shard_map/while/body/eval_jaxpr/dot_general | solution.py:55
  165.7 10.0 %and_select_fusion.4 = (s32[128]{0:T(128)S(1)}, s32[128]{0:T(128)S(1)}) fusion(s32[]{:T(128)} %bitcast.344, s32[]{:T(128)} %bitcast.345, s32[]{:T(128)} %bitcast.346, s32[]{:T(128)} %bitcast.347, s32[]{:T(128)} %bitcast.348, s32[]{:T(128)} %bitcast.349, s32[]{:T(128)} %bitcast.350, s32[]{:T(128)} %bitcast.351, s32[]{:T(128)} %bitcast.352, ...), kind=kLoop, calls=%fused_computation.89.clone.1 | loop fusion | flops 9216 | bytes 1092 | tf_op jit(solution)/shard_map/while/body/eval_jaxpr/jit(_take)/select_n | solution.py:166
  179.5 3.9 %multiply_convert_fusion.4 = bf16[1024,1024]{1,0:T(8,128)(2,1)S(1)} fusion(f32[1024,1024]{1,0:T(8,128)} %fusion.196, bf16[1024,128]{1,0:T(8,128)(2,1)} %get-tuple-element.918, f32[1024]{0:T(1024)S(1)} %sub.266, f32[1024]{0:T(1024)S(1)} %sub.267, pred[128,1024]{1,0:T(8,128)(4,1)} %compare_and_fusion.5, bf16[256,8,128]{2,1,0:T(8,128)(2,1)} %get-tuple-element.917, ...), kind=kOutput, calls=%fused_computation.35.clone.1 | convolution fusion | flops 274726912 | bytes 6955012 | tf_op jit(solution)/shard_map/while/body/eval_jaxpr/dot_general | solution.py:55
  189.2 3.3 %fusion.200 = f32[1024,1,128]{2,0,1:T(8,128)} fusion(f32[1024,1024]{1,0:T(8,128)S(1)} %copy-done.2, f32[1024]{0:T(1024)S(1)} %sub.267, pred[128,1024]{1,0:T(8,128)(4,1)S(1)} %copy-done.9, f32[1024,1,128]{2,0,1:T(8,128)} %get-tuple-element.894, pred[]{:T(512)S(6)} %compare.245, bf16[256,8,128]{2,1,0:T(8,128)(2,1)S(1)} %copy-done.14, s32[]{:T(128)S(6)} %select_n.283), kind=kOutput, calls=%fused_computation.46.clone.1 | convolution fusion | flops 272891904 | bytes 5640197 | tf_op jit(solution)/shard_map/while/body/eval_jaxpr/dot_general | solution.py:66
  192.5 6.7 %scatter_custom_fusion.1 = f32[1024,128]{1,0:T(8,128)} fusion(s32[1024]{0:T(1024)S(1)} %bitcast.386, f32[1024,1,128]{2,0,1:T(8,128)} %get-tuple-element.322, f32[]{:T(128)} %constant.217.clone.1), kind=kCustom, calls=%fused_computation.140 | custom fusion | flops 131072 | bytes 1048580 | tf_op jit(solution)/shard_map/scatter-add | solution.py:196
  199.3 6.8 %scatter_custom_fusion = f32[1024,128]{1,0:T(8,128)} fusion(s32[1024]{0:T(1024)S(1)} %bitcast.387, f32[1024,1,128]{2,0,1:T(8,128)S(1)} %get-tuple-element.320, f32[]{:T(128)} %constant.217.clone.1), kind=kCustom, calls=%fused_computation.142 | custom fusion | flops 131072 | bytes 1048580 | tf_op jit(solution)/shard_map/scatter-add | solution.py:191
  207.6 56.9 %while.50 = (s32[]{:T(128)}, f32[512,1,128]{2,0,1:T(8,128)S(1)}, f32[512,1,128]{2,0,1:T(8,128)}, f32[4,128,8,128]{3,2,1,0:T(8,128)}, s32[4]{0:T(128)S(1)}, /*ind...) while((s32[]{:T(128)}, f32[512,1,128]{2,0,1:T(8,128)S(1)}, ...), condition=%wide.region_4.5_spmd.clone.clone, body=%wide.region_3.4_spmd.clone.clone.sunk | while | flops 675414016 | bytes 13156130 | solution.py:74
  210.1 3.0 %exponential_select_fusion.3 = f32[1024,512]{1,0:T(8,128)} fusion(bf16[512,128]{1,0:T(8,128)(2,1)S(1)} %get-tuple-element.1011, f32[1024]{0:T(1024)S(1)} %sub.272, pred[128,512]{1,0:T(8,128)(4,1)S(1)} %compare_and_fusion.6, bf16[512,8,128]{2,1,0:T(8,128)(2,1)} %get-tuple-element.1010, s32[]{:T(128)S(6)} %select_n.285), kind=kOutput, calls=%fused_computation.105.clone.1 | convolution fusion | flops 135790592 | bytes 2560004 | tf_op jit(solution)/shard_map/while/body/eval_jaxpr/dot_general | solution.py:50
  224.3 3.0 %exponential_select_fusion.3 = f32[1024,512]{1,0:T(8,128)} fusion(bf16[512,128]{1,0:T(8,128)(2,1)S(1)} %get-tuple-element.1011, f32[1024]{0:T(1024)S(1)} %sub.272, pred[128,512]{1,0:T(8,128)(4,1)S(1)} %compare_and_fusion.6, bf16[512,8,128]{2,1,0:T(8,128)(2,1)} %get-tuple-element.1010, s32[]{:T(128)S(6)} %select_n.285), kind=kOutput, calls=%fused_computation.105.clone.1 | convolution fusion | flops 135790592 | bytes 2560004 | tf_op jit(solution)/shard_map/while/body/eval_jaxpr/dot_general | solution.py:50
  233.2 2.9 %fusion.213 = f32[512,1,128]{2,0,1:T(8,128)} fusion(f32[1024,512]{1,0:T(8,128)} %exponential_select_fusion.3, f32[512,1,128]{2,0,1:T(8,128)} %get-tuple-element.988, bf16[512,8,128]{2,1,0:T(8,128)(2,1)} %get-tuple-element.1013, s32[]{:T(128)S(6)} %select_n.285, pred[]{:T(512)S(6)} %compare.246), kind=kOutput, calls=%fused_computation.112.clone.1 | convolution fusion | flops 134873088 | bytes 2883589 | tf_op jit(solution)/shard_map/while/body/eval_jaxpr/dot_general | solution.py:66
  238.6 3.0 %exponential_select_fusion.3 = f32[1024,512]{1,0:T(8,128)} fusion(bf16[512,128]{1,0:T(8,128)(2,1)S(1)} %get-tuple-element.1011, f32[1024]{0:T(1024)S(1)} %sub.272, pred[128,512]{1,0:T(8,128)(4,1)S(1)} %compare_and_fusion.6, bf16[512,8,128]{2,1,0:T(8,128)(2,1)} %get-tuple-element.1010, s32[]{:T(128)S(6)} %select_n.285), kind=kOutput, calls=%fused_computation.105.clone.1 | convolution fusion | flops 135790592 | bytes 2560004 | tf_op jit(solution)/shard_map/while/body/eval_jaxpr/dot_general | solution.py:50
  247.4 2.9 %fusion.213 = f32[512,1,128]{2,0,1:T(8,128)} fusion(f32[1024,512]{1,0:T(8,128)} %exponential_select_fusion.3, f32[512,1,128]{2,0,1:T(8,128)} %get-tuple-element.988, bf16[512,8,128]{2,1,0:T(8,128)(2,1)} %get-tuple-element.1013, s32[]{:T(128)S(6)} %select_n.285, pred[]{:T(512)S(6)} %compare.246), kind=kOutput, calls=%fused_computation.112.clone.1 | convolution fusion | flops 134873088 | bytes 2883589 | tf_op jit(solution)/shard_map/while/body/eval_jaxpr/dot_general | solution.py:66
  252.8 3.0 %exponential_select_fusion.3 = f32[1024,512]{1,0:T(8,128)} fusion(bf16[512,128]{1,0:T(8,128)(2,1)S(1)} %get-tuple-element.1011, f32[1024]{0:T(1024)S(1)} %sub.272, pred[128,512]{1,0:T(8,128)(4,1)S(1)} %compare_and_fusion.6, bf16[512,8,128]{2,1,0:T(8,128)(2,1)} %get-tuple-element.1010, s32[]{:T(128)S(6)} %select_n.285), kind=kOutput, calls=%fused_computation.105.clone.1 | convolution fusion | flops 135790592 | bytes 2560004 | tf_op jit(solution)/shard_map/while/body/eval_jaxpr/dot_general | solution.py:50
  261.7 2.9 %fusion.213 = f32[512,1,128]{2,0,1:T(8,128)} fusion(f32[1024,512]{1,0:T(8,128)} %exponential_select_fusion.3, f32[512,1,128]{2,0,1:T(8,128)} %get-tuple-element.988, bf16[512,8,128]{2,1,0:T(8,128)(2,1)} %get-tuple-element.1013, s32[]{:T(128)S(6)} %select_n.285, pred[]{:T(512)S(6)} %compare.246), kind=kOutput, calls=%fused_computation.112.clone.1 | convolution fusion | flops 134873088 | bytes 2883589 | tf_op jit(solution)/shard_map/while/body/eval_jaxpr/dot_general | solution.py:66
  (226 shorter events, 126.7 us)
Async XLA Ops:
  7.2 262.5 %reduce-scatter.9.cloned.1.call-start = ((), (), s32[]{:S(2)}) async-start(), calls=%async_computation.6 | async-start | bytes 81920 | tf_op jit(solution)/shard_map/reduce_scatter | solution.py:127
  17.7 17.4 %copy-start.17 = (bf16[32,128]{1,0:T(8,128)(2,1)S(1)}, bf16[32,128]{1,0:T(8,128)(2,1)}, u32[]{:S(2)}) copy-start(bf16[32,128]{1,0:T(8,128)(2,1)} %param.28) | copy-start | bytes 24580
  52.2 35.8 %copy-start.19 = (s32[64,1]{0,1:T(1,128)S(1)}, s32[64,1]{0,1:T(1,128)}, u32[]{:S(2)}) copy-start(s32[64,1]{0,1:T(1,128)} %param.29) | copy-start | bytes 772
  52.2 36.5 %copy-start.18 = (s32[64]{0:T(128)S(1)}, s32[64]{0:T(128)}, u32[]{:S(2)}) copy-start(s32[64]{0:T(128)} %param.30) | copy-start | bytes 772
  86.6 21.7 %copy-start.4 = (f32[8,512]{0,1:T(8,128)}, f32[8,512]{0,1:T(8,128)S(1)}, u32[]{:S(2)}) copy-start(f32[8,512]{0,1:T(8,128)S(1)} %get-tuple-element.1025) | copy-start | bytes 49156
  86.6 40.0 %copy-start.5 = (f32[8,512]{0,1:T(8,128)}, f32[8,512]{0,1:T(8,128)S(1)}, u32[]{:S(2)}) copy-start(f32[8,512]{0,1:T(8,128)S(1)} %get-tuple-element.1026) | copy-start | bytes 49156
  86.6 7.5 %slice-start.1 = ((bf16[512,128]{1,0:T(8,128)(2,1)}), bf16[256,128]{1,0:T(8,128)(2,1)S(1)}, s32[]{:S(2)}) async-start(bf16[512,128]{1,0:T(8,128)(2,1)} %param.25), calls=%async_computation.9 | async-start | bytes 131072 | tf_op jit(solution)/shard_map/slice | solution.py:171
  86.6 21.7 %slice-start = ((bf16[512,128]{1,0:T(8,128)(2,1)}), bf16[256,128]{1,0:T(8,128)(2,1)S(1)}, s32[]{:S(2)}) async-start(bf16[512,128]{1,0:T(8,128)(2,1)} %param.26), calls=%async_computation.8 | async-start | bytes 131072 | tf_op jit(solution)/shard_map/slice | solution.py:172
  86.6 184.4 %reduce-scatter.11.cloned.1.call-start = ((), (), s32[]{:S(2)}) async-start(), calls=%async_computation.7 | async-start | bytes 81920 | tf_op jit(solution)/shard_map/reduce_scatter | solution.py:130
  87.4 185.0 %reduce-scatter.7.cloned.1.call-start = ((), (), s32[]{:S(2)}) async-start(), calls=%async_computation.5 | async-start | bytes 655360 | tf_op jit(solution)/shard_map/reduce_scatter | solution.py:200
  126.6 7.4 %copy-start.20 = (s32[64]{0:T(128)S(1)}, s32[64]{0:T(128)}, u32[]{:S(2)}) copy-start(s32[64]{0:T(128)} %param.31) | copy-start | bytes 772
  158.5 2.8 copy-start.2
  158.5 2.8 copy-start.9
  158.5 3.0 %copy-start.14 = (bf16[256,8,128]{2,1,0:T(8,128)(2,1)S(1)}, bf16[256,8,128]{2,1,0:T(8,128)(2,1)}, u32[]{:S(2)}) copy-start(bf16[256,8,128]{2,1,0:T(8,128)(2,1)} %get-tuple-element.917) | copy-start | bytes 1572868 | tf_op jit(solution)/shard_map/while
  186.2 2.8 copy-start.2
  186.2 2.8 copy-start.9
  186.2 3.0 %copy-start.14 = (bf16[256,8,128]{2,1,0:T(8,128)(2,1)S(1)}, bf16[256,8,128]{2,1,0:T(8,128)(2,1)}, u32[]{:S(2)}) copy-start(bf16[256,8,128]{2,1,0:T(8,128)(2,1)} %get-tuple-element.917) | copy-start | bytes 1572868 | tf_op jit(solution)/shard_map/while
  199.2 8.4 %copy-start.6 = (bf16[512,128]{1,0:T(8,128)(2,1)S(1)}, bf16[512,128]{1,0:T(8,128)(2,1)}, u32[]{:S(2)}) copy-start(bf16[512,128]{1,0:T(8,128)(2,1)} %param.26) | copy-start | bytes 393220
  199.2 8.4 %copy-start.7 = (bf16[512,128]{1,0:T(8,128)(2,1)S(1)}, bf16[512,128]{1,0:T(8,128)(2,1)}, u32[]{:S(2)}) copy-start(bf16[512,128]{1,0:T(8,128)(2,1)} %param.25) | copy-start | bytes 393220
  199.2 74.7 %reduce-scatter.5.cloned.1.call-start = ((), (), s32[]{:S(2)}) async-start(), calls=%async_computation.4 | async-start | bytes 655360 | tf_op jit(solution)/shard_map/reduce_scatter | solution.py:199
  219.0 2.8 copy-start.8
  233.2 2.9 %copy-start.8 = (bf16[512,128]{1,0:T(8,128)(2,1)S(1)}, bf16[512,128]{1,0:T(8,128)(2,1)}, u32[]{:S(2)}) copy-start(bf16[512,128]{1,0:T(8,128)(2,1)} %get-tuple-element.1044) | copy-start | bytes 393220 | tf_op jit(solution)/shard_map/while
  247.4 2.9 %copy-start.8 = (bf16[512,128]{1,0:T(8,128)(2,1)S(1)}, bf16[512,128]{1,0:T(8,128)(2,1)}, u32[]{:S(2)}) copy-start(bf16[512,128]{1,0:T(8,128)(2,1)} %get-tuple-element.1044) | copy-start | bytes 393220 | tf_op jit(solution)/shard_map/while
  261.7 2.9 %copy-start.8 = (bf16[512,128]{1,0:T(8,128)(2,1)S(1)}, bf16[512,128]{1,0:T(8,128)(2,1)}, u32[]{:S(2)}) copy-start(bf16[512,128]{1,0:T(8,128)(2,1)} %get-tuple-element.1044) | copy-start | bytes 393220 | tf_op jit(solution)/shard_map/while
  (12 other events, 23.9 us)
Sparse Core Ops, SparseCore 0:
  86.8 20.0 reduce-scatter.8
  109.2 17.1 reduce-scatter.10
  199.3 23.3 reduce-scatter.6
  224.8 19.8 reduce-scatter.4
where the time goes:
time: 284 us; the launch traced here: 282 us
  matrix products  106 us (37%)
  blocking collectives  56.1 us (20%)
  other arithmetic  51.8 us (18%)
  local copies, waits for them, and re-layouts  45.9 us (16%)
  between operations  14 us (5%)
  loops' own time  6.92 us (2%)
    dot_general x10, matrix products, block_step(): lax.dot_general(weights_low, out_flat, across, preferred_element_type=jnp...  24.4 us
    dot_general x10, matrix products, block_step(): lax.dot_general(query_flat, key_list[0], contract, preferred_element_type...  22.1 us
    dot_general x10, matrix products, block_step(): lax.dot_general(out_flat, value_list[0], contract, preferred_element_type...  21.1 us
    select_n x2, other arithmetic, parent_rows(): child_limit = jnp.take(my_offsets, child_ids, axis=0)  20.1 us
    dot_general x10, matrix products, block_step(): lax.dot_general(score_grads, query_flat, across, preferred_element_type=j...  18.6 us
    unnamed x39, local copies, waits for them, and re-layouts  15.8 us
    dot_general x10, matrix products, block_step(): jnp.dot(score_grads, key_list[0], preferred_element_type=jnp.float32)  15.7 us
    all_gather x1, blocking collectives, local(): lax.all_gather(prefix_keys, 'servers', axis=0, tiled=True)  14.8 us
  transfers between devices with their start and end apart: 4, of which 0 were waited for; matrix products, arithmetic and copies ran while one was open for 53% of the time, Pallas kernels for 0%

commit v1 on v0

--- a/solution.py
+++ b/solution.py
@@ -1,3 +1,4 @@
+import functools
 import math
 import jax
 import jax.numpy as jnp
@@ -9,6 +10,39 @@
 ROOTS_DEV = 4
 RLEN = 64
 CLEN = 16
+
+
+def cover_series_all(frame_in, which_axis, k_dim):
+    step_out, top, found_now = (
+        lax.axis_size(which_axis),
+        lax.axis_index(which_axis),
+        frame_in.shape[k_dim],
+    )
+    shelf = [jj * step_out if num == k_dim else jj for num, jj in enumerate(frame_in.shape)]
+    high = lax.dynamic_update_slice_in_dim(
+        jnp.zeros(shelf, frame_in.dtype), frame_in, top * found_now, axis=k_dim
+    )
+    s_next = earlier = frame_in
+    for ii in range(1, step_out // 2 + 1):
+        s_next = lax.ppermute(
+            s_next, which_axis, list(map(lambda num: (num, (num + 1) % step_out), range(step_out)))
+        )
+        high = lax.dynamic_update_slice_in_dim(
+            high, s_next, (top - ii) % step_out * found_now, axis=k_dim
+        )
+        if 2 * ii < step_out:
+            earlier = lax.ppermute(
+                earlier,
+                which_axis,
+                list(map(lambda num: (num, (num - 1) % step_out), range(step_out))),
+            )
+            high = lax.dynamic_update_slice_in_dim(
+                high, earlier, (top + ii) % step_out * found_now, axis=k_dim
+            )
+    return high
+
+
+_note_unit = functools.partial(cover_series_all, which_axis="servers", k_dim=0)
 
 
 def attend(query_heads, out_heads, lse_rows, delta_rows, key_heads, value_heads, mask_rows):
@@ -170,10 +204,7 @@
 
     root_keys = keys[:root_rows]
     root_values = values[:root_rows]
-    all_roots = (
-        lax.all_gather(root_keys, "servers", axis=0, tiled=True),
-        lax.all_gather(root_values, "servers", axis=0, tiled=True),
-    )
+    all_roots = (_note_unit(root_keys), lax.all_gather(root_values, "servers", axis=0, tiled=True))
     parent_index = ((my_owners * ROOTS_DEV + my_roots) * RLEN)[:, None] + positions[None, :]
     flat_index = parent_index.reshape(-1)
     parent_keys = jnp.take(all_roots[0], flat_index, axis=0).reshape(

time: 284 us -> 295 us (1.039)
  blocking collectives: 56.1 us -> 41.7 us
  waiting for transfers between devices: 0.77 us -> 11.5 us
  local copies, waits for them, and re-layouts: 45.9 us -> 54.9 us
  starting transfers between devices: 0.16 us -> 4.5 us
    all_gather x1 -> x0, blocking collectives: 14.2 us -> none  [local(): lax.all_gather(root_keys, 'servers', axis=0, tiled=True)]
    reduce_scatter x1, waiting for transfers between devices: 0.01 us -> 6.89 us  [local(): lax.psum_scatter(dense_keys, 'servers', scatter_dimension=0, tiled=True)]
    ppermute x0 -> x3, waiting for transfers between devices: none -> 4.52 us  [the longest x2 4.52 us: cover_series_all(): lax.ppermute(s_next, which_axis, list(map(lambda num: (num, (num + 1) % s...]
    ppermute x0 -> x3, starting transfers between devices: none -> 4.11 us  [the longest x1 2.3 us: cover_series_all(): lax.ppermute(earlier, which_axis, list(map(lambda num: (num, (num - 1) %...]
    unnamed x39 -> x47, local copies, waits for them, and re-layouts: 15.8 us -> 17.7 us
  transfers between devices with their start and end apart: 4 -> 7, of which waited for: 0 -> 2; matrix products, arithmetic and copies ran while one was open for 53% -> 56% of each run, Pallas kernels for 0% -> 0%
where the time goes in v1:
time: 295 us; the launch traced here: 292 us
  matrix products  106 us (36%)
  local copies, waits for them, and re-layouts  54.9 us (19%)
  other arithmetic  52.8 us (18%)
  blocking collectives  41.7 us (14%)
  between operations  14.1 us (5%)
  waiting for transfers between devices  11.5 us (4%)
  loops' own time  7.07 us (2%)
  starting transfers between devices  4.5 us (2%)
    dot_general x10, matrix products, block_step(): lax.dot_general(weights_low, out_flat, across, preferred_element_type=jnp...  24.5 us
    dot_general x10, matrix products, block_step(): lax.dot_general(query_flat, key_list[0], contract, preferred_element_type...  24 us
    dot_general x10, matrix products, block_step(): lax.dot_general(out_flat, value_list[0], contract, preferred_element_type...  20.9 us
    select_n x2, other arithmetic, parent_rows(): child_limit = jnp.take(my_offsets, child_ids, axis=0)  19.9 us
    unnamed x47, local copies, waits for them, and re-layouts  17.7 us
    dot_general x10, matrix products, block_step(): lax.dot_general(score_grads, query_flat, across, preferred_element_type=j...  16.2 us
    dot_general x10, matrix products, block_step(): jnp.dot(score_grads, key_list[0], preferred_element_type=jnp.float32)  15.8 us
    all_gather x1, blocking collectives, local(): lax.all_gather(prefix_values, 'servers', axis=0, tiled=True)  14.8 us
  transfers between devices with their start and end apart: 7, of which 2 were waited for; matrix products, arithmetic and copies ran while one was open for 56% of the time, Pallas kernels for 0%

profile of v1, /device:TPU:0, one launch (start us, length us, event | category | flops | bytes accessed | tf_op | source)
XLA Modules:
  0.0 292.3 jit_solution(14036632177774455483)
XLA Ops:
  8.8 4.5 %convolution_convert_fusion = bf16[512,1024]{1,0:T(8,128)(2,1)S(1)} fusion(bf16[512,2048]{1,0:T(8,128)(2,1)S(1)} %copy-done, bf16[2048,1024]{1,0:T(8,128)(2,1)} %param.21), kind=kOutput, calls=%fused_computation.132 | convolution fusion | flops 2148007936 | bytes 7340032 | tf_op jit(solution)/shard_map/dot_general | solution.py:135
  19.1 14.8 %all_gather.10 = bf16[128,128]{1,0:T(8,128)(2,1)S(1)} all-gather(bf16[32,128]{1,0:T(8,128)(2,1)S(1)} %copy-done.19), channel_id=1, replica_groups=mesh['groups'=2,'servers'=4,'heads'=4] {'servers'}, dimensions={0}, use_global_device_ids=true | all-gather | bytes 40960 | tf_op jit(solution)/shard_map/all_gather | solution.py:148
  33.9 13.1 %all_gather.9 = bf16[128,128]{1,0:T(8,128)(2,1)S(1)} all-gather(bf16[32,128]{1,0:T(8,128)(2,1)S(1)} %copy-done.20), channel_id=1, replica_groups=mesh['groups'=2,'servers'=4,'heads'=4] {'servers'}, dimensions={0}, use_global_device_ids=true | all-gather | bytes 40960 | tf_op jit(solution)/shard_map/all_gather | solution.py:147
  51.0 31.9 %while.48 = (s32[]{:T(128)}, f32[128,1,128]{2,0,1:T(8,128)S(1)}, f32[128,1,128]{2,0,1:T(8,128)}, f32[4,128,8,128]{3,2,1,0:T(8,128)}, s32[4]{0:T(128)S(1)}, /*ind...) while((s32[]{:T(128)}, f32[128,1,128]{2,0,1:T(8,128)S(1)}, ...), condition=%wide.region_2.3_spmd.clone, body=%wide.region_1.2_spmd.clone.sunk | while | flops 168771584 | bytes 4334310 | solution.py:108
  96.8 13.8 %all_gather.11 = bf16[1024,128]{1,0:T(8,128)(2,1)S(1)} all-gather(bf16[256,128]{1,0:T(8,128)(2,1)S(1)} %slice-done), channel_id=1, replica_groups=mesh['groups'=2,'servers'=4,'heads'=4] {'servers'}, dimensions={0}, use_global_device_ids=true | all-gather | bytes 327680 | tf_op jit(solution)/shard_map/all_gather | solution.py:207
  115.1 3.2 %gather_fusion.1 = bf16[1024,128]{1,0:T(8,128)(2,1)S(1)} fusion(bf16[1024,128]{1,0:T(8,128)(2,1)S(1)} %all_gather.11, s32[1024]{0:T(1024)S(1)} %fusion.100), kind=kCustom, calls=%fused_computation.1.clone | custom fusion | bytes 528384 | tf_op jit(solution)/shard_map/jit(_take)/gather | solution.py:213
  120.4 4.5 %collective-permute-done.2 = bf16[256,128]{1,0:T(8,128)(2,1)S(1)} collective-permute-done((bf16[256,128]{1,0:T(8,128)(2,1)}, bf16[256,128]{1,0:T(8,128)(2,1)S(1)}, u32[]{:S(2)}, u32[]{:S(2)}) %collective-permute-start.2) | collective-permute-done | bytes 65568 | tf_op jit(solution)/shard_map/ppermute | solution.py:27
  125.0 4.3 %gather_fusion = bf16[1024,128]{1,0:T(8,128)(2,1)} fusion(bf16[1024,128]{1,0:T(8,128)(2,1)S(1)} %constant_dynamic-update-slice_fusion, s32[1024]{0:T(1024)S(1)} %fusion.100), kind=kCustom, calls=%fused_computation.clone | custom fusion | bytes 528384 | tf_op jit(solution)/shard_map/jit(_take)/gather | solution.py:210
  131.6 60.0 %while.49 = (s32[]{:T(128)}, f32[1024,1,128]{2,0,1:T(8,128)S(1)}, f32[1024,1,128]{2,0,1:T(8,128)}, f32[2,128,8,128]{3,2,1,0:T(8,128)}, s32[2]{0:T(128)}, /*index...) while((s32[]{:T(128)}, f32[1024,1,128]{2,0,1:T(8,128)S(1)}, ...), condition=%wide.region_6.8_spmd.clone, body=%wide.region_5.7_spmd.clone.sunk | while | flops 1353864192 | bytes 54197308 | solution.py:108
  134.3 10.0 %and_select_fusion.4 = (s32[128]{0:T(128)S(1)}, s32[128]{0:T(128)S(1)}) fusion(s32[]{:T(128)} %bitcast.344, s32[]{:T(128)} %bitcast.345, s32[]{:T(128)} %bitcast.346, s32[]{:T(128)} %bitcast.347, s32[]{:T(128)} %bitcast.348, s32[]{:T(128)} %bitcast.349, s32[]{:T(128)} %bitcast.350, s32[]{:T(128)} %bitcast.351, s32[]{:T(128)} %bitcast.352, ...), kind=kLoop, calls=%fused_computation.89.clone.1 | loop fusion | flops 9216 | bytes 1092 | tf_op jit(solution)/shard_map/while/body/eval_jaxpr/jit(_take)/select_n | solution.py:200
  144.4 3.7 %fusion.199 = f32[1024,1024]{1,0:T(8,128)} fusion(bf16[1024,128]{1,0:T(8,128)(2,1)S(1)} %get-tuple-element.917, bf16[256,8,128]{2,1,0:T(8,128)(2,1)} %get-tuple-element.916, s32[]{:T(128)S(6)} %select_n.316), kind=kOutput, calls=%fused_computation.52.clone.1 | convolution fusion | flops 268435456 | bytes 4718596 | tf_op jit(solution)/shard_map/while/body/eval_jaxpr/dot_general | solution.py:84
  149.2 3.8 %multiply_convert_fusion.4 = bf16[1024,1024]{1,0:T(8,128)(2,1)S(1)} fusion(f32[1024,1024]{1,0:T(8,128)} %fusion.199, bf16[1024,128]{1,0:T(8,128)(2,1)S(1)} %copy-done.17, f32[1024]{0:T(1024)S(1)} %sub.274, f32[1024]{0:T(1024)S(1)} %sub.275, pred[128,1024]{1,0:T(8,128)(4,1)S(1)} %compare_and_fusion.5, bf16[256,8,128]{2,1,0:T(8,128)(2,1)} %get-tuple-element.919, ...), kind=kOutput, calls=%fused_computation.35.clone.1 | convolution fusion | flops 274726912 | bytes 6955012 | tf_op jit(solution)/shard_map/while/body/eval_jaxpr/dot_general | solution.py:89
  163.7 10.0 %and_select_fusion.4 = (s32[128]{0:T(128)S(1)}, s32[128]{0:T(128)S(1)}) fusion(s32[]{:T(128)} %bitcast.344, s32[]{:T(128)} %bitcast.345, s32[]{:T(128)} %bitcast.346, s32[]{:T(128)} %bitcast.347, s32[]{:T(128)} %bitcast.348, s32[]{:T(128)} %bitcast.349, s32[]{:T(128)} %bitcast.350, s32[]{:T(128)} %bitcast.351, s32[]{:T(128)} %bitcast.352, ...), kind=kLoop, calls=%fused_computation.89.clone.1 | loop fusion | flops 9216 | bytes 1092 | tf_op jit(solution)/shard_map/while/body/eval_jaxpr/jit(_take)/select_n | solution.py:200
  173.9 3.7 %fusion.199 = f32[1024,1024]{1,0:T(8,128)} fusion(bf16[1024,128]{1,0:T(8,128)(2,1)S(1)} %get-tuple-element.917, bf16[256,8,128]{2,1,0:T(8,128)(2,1)} %get-tuple-element.916, s32[]{:T(128)S(6)} %select_n.316), kind=kOutput, calls=%fused_computation.52.clone.1 | convolution fusion | flops 268435456 | bytes 4718596 | tf_op jit(solution)/shard_map/while/body/eval_jaxpr/dot_general | solution.py:84
  178.6 3.8 %multiply_convert_fusion.4 = bf16[1024,1024]{1,0:T(8,128)(2,1)S(1)} fusion(f32[1024,1024]{1,0:T(8,128)} %fusion.199, bf16[1024,128]{1,0:T(8,128)(2,1)S(1)} %copy-done.17, f32[1024]{0:T(1024)S(1)} %sub.274, f32[1024]{0:T(1024)S(1)} %sub.275, pred[128,1024]{1,0:T(8,128)(4,1)S(1)} %compare_and_fusion.5, bf16[256,8,128]{2,1,0:T(8,128)(2,1)} %get-tuple-element.919, ...), kind=kOutput, calls=%fused_computation.35.clone.1 | convolution fusion | flops 274726912 | bytes 6955012 | tf_op jit(solution)/shard_map/while/body/eval_jaxpr/dot_general | solution.py:89
  188.3 3.3 %fusion.203 = f32[1024,1,128]{2,0,1:T(8,128)} fusion(f32[1024,1024]{1,0:T(8,128)S(1)} %copy-done.2, f32[1024]{0:T(1024)S(1)} %sub.275, pred[128,1024]{1,0:T(8,128)(4,1)S(1)} %compare_and_fusion.5, f32[1024,1,128]{2,0,1:T(8,128)} %get-tuple-element.896, pred[]{:T(512)S(6)} %compare.248, bf16[256,8,128]{2,1,0:T(8,128)(2,1)S(1)} %copy-done.16, ...), kind=kOutput, calls=%fused_computation.46.clone.1 | convolution fusion | flops 272891904 | bytes 5640197 | tf_op jit(solution)/shard_map/while/body/eval_jaxpr/dot_general | solution.py:100
  191.6 6.9 %scatter_custom_fusion.1 = f32[1024,128]{1,0:T(8,128)} fusion(s32[1024]{0:T(1024)} %bitcast.388, f32[1024,1,128]{2,0,1:T(8,128)} %get-tuple-element.322, f32[]{:T(128)} %constant.242.clone.1), kind=kCustom, calls=%fused_computation.140 | custom fusion | flops 131072 | bytes 1049088 | tf_op jit(solution)/shard_map/scatter-add | solution.py:227
  200.4 57.1 %while.50 = (s32[]{:T(128)}, f32[512,1,128]{2,0,1:T(8,128)S(1)}, f32[512,1,128]{2,0,1:T(8,128)}, f32[4,128,8,128]{3,2,1,0:T(8,128)}, s32[4]{0:T(128)S(1)}, /*ind...) while((s32[]{:T(128)}, f32[512,1,128]{2,0,1:T(8,128)S(1)}, ...), condition=%wide.region_4.5_spmd.clone.clone, body=%wide.region_3.4_spmd.clone.clone.sunk | while | flops 675414016 | bytes 13156314 | solution.py:108
  202.9 2.9 %exponential_select_fusion.3 = f32[1024,512]{1,0:T(8,128)} fusion(bf16[512,128]{1,0:T(8,128)(2,1)S(1)} %get-tuple-element.1013, f32[1024]{0:T(1024)S(1)} %sub.280, pred[128,512]{1,0:T(8,128)(4,1)S(1)} %compare_and_fusion.6, bf16[512,8,128]{2,1,0:T(8,128)(2,1)} %get-tuple-element.1012, s32[]{:T(128)S(6)} %select_n.318), kind=kOutput, calls=%fused_computation.105.clone.1 | convolution fusion | flops 135790592 | bytes 2560004 | tf_op jit(solution)/shard_map/while/body/eval_jaxpr/dot_general | solution.py:84
  217.1 3.0 %exponential_select_fusion.3 = f32[1024,512]{1,0:T(8,128)} fusion(bf16[512,128]{1,0:T(8,128)(2,1)S(1)} %get-tuple-element.1013, f32[1024]{0:T(1024)S(1)} %sub.280, pred[128,512]{1,0:T(8,128)(4,1)S(1)} %compare_and_fusion.6, bf16[512,8,128]{2,1,0:T(8,128)(2,1)} %get-tuple-element.1012, s32[]{:T(128)S(6)} %select_n.318), kind=kOutput, calls=%fused_computation.105.clone.1 | convolution fusion | flops 135790592 | bytes 2560004 | tf_op jit(solution)/shard_map/while/body/eval_jaxpr/dot_general | solution.py:84
  231.4 2.9 %exponential_select_fusion.3 = f32[1024,512]{1,0:T(8,128)} fusion(bf16[512,128]{1,0:T(8,128)(2,1)S(1)} %get-tuple-element.1013, f32[1024]{0:T(1024)S(1)} %sub.280, pred[128,512]{1,0:T(8,128)(4,1)S(1)} %compare_and_fusion.6, bf16[512,8,128]{2,1,0:T(8,128)(2,1)} %get-tuple-element.1012, s32[]{:T(128)S(6)} %select_n.318), kind=kOutput, calls=%fused_computation.105.clone.1 | convolution fusion | flops 135790592 | bytes 2560004 | tf_op jit(solution)/shard_map/while/body/eval_jaxpr/dot_general | solution.py:84
  245.7 2.9 %exponential_select_fusion.3 = f32[1024,512]{1,0:T(8,128)} fusion(bf16[512,128]{1,0:T(8,128)(2,1)S(1)} %get-tuple-element.1013, f32[1024]{0:T(1024)S(1)} %sub.280, pred[128,512]{1,0:T(8,128)(4,1)S(1)} %compare_and_fusion.6, bf16[512,8,128]{2,1,0:T(8,128)(2,1)} %get-tuple-element.1012, s32[]{:T(128)S(6)} %select_n.318), kind=kOutput, calls=%fused_computation.105.clone.1 | convolution fusion | flops 135790592 | bytes 2560004 | tf_op jit(solution)/shard_map/while/body/eval_jaxpr/dot_general | solution.py:84
  257.5 6.7 %scatter_custom_fusion = f32[1024,128]{1,0:T(8,128)} fusion(s32[1024]{0:T(1024)} %bitcast.389, f32[1024,1,128]{2,0,1:T(8,128)} %copy-done.3, f32[]{:T(128)} %constant.242.clone.1), kind=kCustom, calls=%fused_computation.142 | custom fusion | flops 131072 | bytes 1049088 | tf_op jit(solution)/shard_map/scatter-add | solution.py:222
  277.3 6.9 %reduce-scatter.5.cloned.1.call-done = f32[256,128]{1,0:T(8,128)} async-done(((f32[1024,128]{1,0:T(8,128)}), f32[256,128]{1,0:T(8,128)}) %reduce-scatter.5.cloned.1.call-update) | async-done | bytes 131088 | tf_op jit(solution)/shard_map/reduce_scatter | solution.py:230
  (254 shorter events, 142.4 us)
Async XLA Ops:
  7.2 263.6 %reduce-scatter.9.cloned.1.call-start = ((), (), s32[]{:S(2)}) async-start(), calls=%async_computation.6 | async-start | bytes 81920 | tf_op jit(solution)/shard_map/reduce_scatter | solution.py:161
  17.7 16.2 %copy-start.20 = (bf16[32,128]{1,0:T(8,128)(2,1)S(1)}, bf16[32,128]{1,0:T(8,128)(2,1)}, u32[]{:S(2)}) copy-start(bf16[32,128]{1,0:T(8,128)(2,1)} %param.27) | copy-start | bytes 24580
  51.0 38.1 %copy-start.22 = (s32[64,1]{0,1:T(1,128)S(1)}, s32[64,1]{0,1:T(1,128)}, u32[]{:S(2)}) copy-start(s32[64,1]{0,1:T(1,128)} %param.29) | copy-start | bytes 772
  51.0 38.9 %copy-start.21 = (s32[64]{0:T(128)S(1)}, s32[64]{0:T(128)}, u32[]{:S(2)}) copy-start(s32[64]{0:T(128)} %param.30) | copy-start | bytes 772
  83.0 29.6 %copy-start.7 = (f32[8,512]{0,1:T(8,128)}, f32[8,512]{0,1:T(8,128)S(1)}, u32[]{:S(2)}) copy-start(f32[8,512]{0,1:T(8,128)S(1)} %get-tuple-element.1027) | copy-start | bytes 49156
  83.0 13.8 %slice-start = ((bf16[512,128]{1,0:T(8,128)(2,1)}), bf16[256,128]{1,0:T(8,128)(2,1)S(1)}, s32[]{:S(2)}) async-start(bf16[512,128]{1,0:T(8,128)(2,1)} %param.26), calls=%async_computation.8 | async-start | bytes 131072 | tf_op jit(solution)/shard_map/slice | solution.py:206
  83.6 188.5 %reduce-scatter.11.cloned.1.call-start = ((), (), s32[]{:S(2)}) async-start(), calls=%async_computation.7 | async-start | bytes 81920 | tf_op jit(solution)/shard_map/reduce_scatter | solution.py:164
  84.6 33.8 %collective-permute-start = (bf16[256,128]{1,0:T(8,128)(2,1)S(1)}, bf16[256,128]{1,0:T(8,128)(2,1)}, u32[]{:S(2)}, u32[]{:S(2)}) collective-permute-start(bf16[256,128]{1,0:T(8,128)(2,1)S(1)} %get-tuple-element.601), channel_id=1, source_target_pairs={{0,4},{4,8},{8,12},{12,0},{1,5},{5,9},{9,13},{13,1},{2,6},{6,10},{... | collective-permute-start | bytes 196616 | tf_op jit(solution)/shard_map/ppermute | solution.py:27
  86.2 33.4 %collective-permute-start.1 = (bf16[256,128]{1,0:T(8,128)(2,1)S(1)}, bf16[256,128]{1,0:T(8,128)(2,1)}, u32[]{:S(2)}, u32[]{:S(2)}) collective-permute-start(bf16[256,128]{1,0:T(8,128)(2,1)S(1)} %get-tuple-element.601), channel_id=1, source_target_pairs={{0,12},{4,0},{8,4},{12,8},{1,13},{5,1},{9,5},{13,9},{2,14},{6,2},{... | collective-permute-start | bytes 196616 | tf_op jit(solution)/shard_map/ppermute | solution.py:34
  88.5 187.2 %reduce-scatter.7.cloned.1.call-start = ((), (), s32[]{:S(2)}) async-start(), calls=%async_computation.5 | async-start | bytes 655360 | tf_op jit(solution)/shard_map/reduce_scatter | solution.py:231
  110.6 7.7 %copy-start.23 = (s32[64]{0:T(128)S(1)}, s32[64]{0:T(128)}, u32[]{:S(2)}) copy-start(s32[64]{0:T(128)} %param.31) | copy-start | bytes 772
  118.5 6.5 %collective-permute-start.2 = (bf16[256,128]{1,0:T(8,128)(2,1)}, bf16[256,128]{1,0:T(8,128)(2,1)S(1)}, u32[]{:S(2)}, u32[]{:S(2)}) collective-permute-start(bf16[256,128]{1,0:T(8,128)(2,1)} %collective-permute-done), channel_id=1, source_target_pairs={{0,4},{4,8},{8,12},{12,0},{1,5},{5,9},{9,13},{13,1},{2,6},{6,10},{... | collective-permute-start | bytes 196616 | tf_op jit(solution)/shard_map/ppermute | solution.py:27
  144.4 4.8 %copy-start.17 = (bf16[1024,128]{1,0:T(8,128)(2,1)S(1)}, bf16[1024,128]{1,0:T(8,128)(2,1)}, u32[]{:S(2)}) copy-start(bf16[1024,128]{1,0:T(8,128)(2,1)} %get-tuple-element.920) | copy-start | bytes 786436 | tf_op jit(solution)/shard_map/while
  173.9 4.7 %copy-start.17 = (bf16[1024,128]{1,0:T(8,128)(2,1)S(1)}, bf16[1024,128]{1,0:T(8,128)(2,1)}, u32[]{:S(2)}) copy-start(bf16[1024,128]{1,0:T(8,128)(2,1)} %get-tuple-element.920) | copy-start | bytes 786436 | tf_op jit(solution)/shard_map/while
  191.6 8.8 %copy-start.3 = (f32[1024,1,128]{2,0,1:T(8,128)}, f32[1024,1,128]{2,0,1:T(8,128)S(1)}, u32[]{:S(2)}) copy-start(f32[1024,1,128]{2,0,1:T(8,128)S(1)} %get-tuple-element.320) | copy-start | bytes 1572868
  191.6 8.7 %copy-start.5 = (f32[512,1,128]{2,0,1:T(8,128)S(1)}, f32[512,1,128]{2,0,1:T(8,128)}, u32[]{:S(2)}) copy-start(f32[512,1,128]{2,0,1:T(8,128)} %custom-call.4) | copy-start | bytes 786436
  191.6 8.7 %copy-start.9 = (bf16[512,128]{1,0:T(8,128)(2,1)S(1)}, bf16[512,128]{1,0:T(8,128)(2,1)}, u32[]{:S(2)}) copy-start(bf16[512,128]{1,0:T(8,128)(2,1)} %param.26) | copy-start | bytes 393220
  191.6 8.7 %copy-start.10 = (bf16[512,128]{1,0:T(8,128)(2,1)S(1)}, bf16[512,128]{1,0:T(8,128)(2,1)}, u32[]{:S(2)}) copy-start(bf16[512,128]{1,0:T(8,128)(2,1)} %param.25) | copy-start | bytes 393220
  198.6 85.6 %reduce-scatter.5.cloned.1.call-start = ((), (), s32[]{:S(2)}) async-start(), calls=%async_computation.4 | async-start | bytes 655360 | tf_op jit(solution)/shard_map/reduce_scatter | solution.py:230
  210.2 4.4 %copy-start.25 = (s32[4]{0:T(128)S(1)}, s32[4]{0:T(128)}, u32[]{:S(2)}) copy-start(s32[4]{0:T(128)} %copy-done.24) | copy-start | bytes 52 | tf_op jit(solution)/shard_map/while
  224.5 4.4 %copy-start.25 = (s32[4]{0:T(128)S(1)}, s32[4]{0:T(128)}, u32[]{:S(2)}) copy-start(s32[4]{0:T(128)} %copy-done.24) | copy-start | bytes 52 | tf_op jit(solution)/shard_map/while
  238.8 4.4 %copy-start.25 = (s32[4]{0:T(128)S(1)}, s32[4]{0:T(128)}, u32[]{:S(2)}) copy-start(s32[4]{0:T(128)} %copy-done.24) | copy-start | bytes 52 | tf_op jit(solution)/shard_map/while
  253.0 4.4 %copy-start.25 = (s32[4]{0:T(128)S(1)}, s32[4]{0:T(128)}, u32[]{:S(2)}) copy-start(s32[4]{0:T(128)} %copy-done.24) | copy-start | bytes 52 | tf_op jit(solution)/shard_map/while
  269.9 5.8 %copy-start.6 = (f32[512,1,128]{2,0,1:T(8,128)S(1)}, f32[512,1,128]{2,0,1:T(8,128)}, u32[]{:S(2)}) copy-start(f32[512,1,128]{2,0,1:T(8,128)} %get-tuple-element.1031) | copy-start | bytes 786436
  (24 other events, 48.1 us)
Sparse Core Ops, SparseCore 0:
  83.7 20.0 reduce-scatter.8
  106.2 17.1 reduce-scatter.10
  198.7 19.9 reduce-scatter.6
  264.3 19.8 reduce-scatter.4
